TPU v7x, 32 devices: a whole 2x2x4 slice. The times are simulated.
32 devices in a mesh: row: 8 (over z, y), col: 4 (over x, core).
Axes of the slice: x: 2, y: 2, z: 4, core: 2. Of those that a mesh axis runs over, the one named last changes fastest.
Arguments:
- tensor_ri: bfloat16 [8, 8, 4, 128, 1152], P('row', None, 'col'), may hold values from -6 to 6
- block_mask: int32 [8, 4, 9], P('row', 'col'), may hold values 0 or 1
- green_virt: bfloat16 [8, 4, 128, 3200], P('row', 'col'), may hold values from -0.1875 to 0.1875
- green_occ: bfloat16 [8, 4, 128, 128], P('row', 'col'), may hold values from -0.5 to 0.5
Outputs:
- response: float32 [8, 8], replicated
All inputs are finite; a program needn't handle non-finite values. No bound on the sum of `block_mask` on one device may be relied on, other than what follows from the above.
Results may differ from a plain program's by a relative error of at most 0.0044.
Values may be sent and summed in bfloat16 or wider, within the bound.
A program may use at most 192 MiB of HBM per device.

v0:
```python
import math
import jax
import jax.numpy as jnp
from jax import lax
from jax.sharding import PartitionSpec as P


def extended(cells, sides, width):
    for axis, dim in sides:
        count = lax.axis_size(axis)
        ends = count - 1
        head = lax.slice_in_dim(cells, 0, width, axis=dim)
        tail = lax.slice_in_dim(cells, cells.shape[dim] - width, cells.shape[dim], axis=dim)
        cells = jnp.concatenate(
            [
                lax.ppermute(tail, axis, [(i, (i + 1) % count) for i in range(ends)]),
                cells,
                lax.ppermute(head, axis, [((i + 1) % count, i) for i in range(ends)]),
            ],
            axis=dim,
        )
    return cells


def window_of(band, src_row, src_col, block_width):
    grid_band = band.reshape(block_width, 5, 5, block_width)
    picked = grid_band[:, 2 - src_row : 5 - src_row, 2 - src_col : 5 - src_col, :]
    return picked.reshape(block_width, 9 * block_width)


def per_device(tensor_ri, block_mask, green_virt, green_occ):
    row_count = lax.axis_size("row")
    col_count = lax.axis_size("col")
    block_width = green_occ.shape[-1]
    pair_width = tensor_ri.shape[-1]
    occ_block = green_occ[0, 0]
    regrouped = lax.all_to_all(tensor_ri, "row", split_axis=1, concat_axis=0, tiled=True)
    occ_applied = jnp.einsum(
        "ji,pabiw->pabjw", occ_block, regrouped, preferred_element_type=jnp.float32
    ).astype(jnp.bfloat16)
    rows_all = regrouped.shape[0]
    regrouped = regrouped.reshape(rows_all, block_width, pair_width)
    occ_applied = occ_applied.reshape(rows_all, block_width, pair_width)
    grid_row = lax.axis_index("row")
    grid_col = lax.axis_index("col")
    slots = jnp.arange(9, dtype=jnp.int32)
    near_row = grid_row + slots // 3 - 1
    near_col = grid_col + slots % 3 - 1
    usable = (
        (block_mask[0, 0] == 1)
        & (near_row >= 0)
        & (near_row < row_count)
        & (near_col >= 0)
        & (near_col < col_count)
    )
    kept_slots = jnp.repeat(usable.astype(jnp.bfloat16), block_width)
    regrouped = regrouped * kept_slots
    occ_applied = occ_applied * kept_slots
    windows = []
    rim_blocks = extended(green_virt, (("row", 0), ("col", 1)), 1)
    for source in range(9):
        src_row, src_col = (source // 3, source % 3)
        windows.append(window_of(rim_blocks[src_row, src_col], src_row, src_col, block_width))
    flat_rows = regrouped.reshape(rows_all * block_width, pair_width)
    half_sum = jnp.zeros((rows_all * block_width, pair_width), jnp.float32)
    for source in range(9):
        tile = flat_rows[:, source * block_width : (source + 1) * block_width]
        half_sum = half_sum + jnp.dot(tile, windows[source], preferred_element_type=jnp.float32)
    half_done = half_sum.astype(jnp.bfloat16).reshape(rows_all, block_width * pair_width)
    occ_flat = occ_applied.reshape(rows_all, block_width * pair_width)
    partial_value = lax.dot_general(
        half_done, occ_flat, (((1,), (1,)), ((), ())), preferred_element_type=jnp.float32
    )
    total_basis = block_width * row_count * col_count
    response = lax.psum(partial_value, ("row", "col"))
    return response * (1.0 / math.sqrt(total_basis * 9 * block_width))


def solution(mesh):
    return jax.shard_map(
        per_device,
        mesh=mesh,
        in_specs=(
            P("row", None, "col", None, None),
            P("row", "col", None),
            P("row", "col", None, None),
            P("row", "col", None, None),
        ),
        out_specs=P(),
        check_vma=False,
    )
```

profile of v0, /device:TPU:10, one launch (start us, length us, event | category | flops | bytes accessed | tf_op | source)
XLA Modules:
  0.0 181.1 jit_solution(1390845295951888833)
XLA Ops:
  0.0 1.7 copy.15
  1.7 3.4 %collective-permute-start.1 = (bf16[1,1,128,3200]{2,3,1,0:T(8,128)(2,1)S(1)}, bf16[1,1,128,3200]{2,3,1,0:T(8,128)(2,1)S(1)}, u32[]{:S(2)}, u32[]{:S(2)}) collective-permute-start(bf16[1,1,128,3200]{2,3,1,0:T(8,128)(2,1)S(1)} %copy.15), channel_id=1, source_target_pairs={{4,0},{8,4},{12,8},{16,12},{20,16},{24,20},{28,24},{5,1},{9,5},{13... | collective-permute-start | bytes 2457608 | tf_op jit(solution)/shard_map/ppermute | solution.py:18
  5.2 2.5 %collective-permute-start = (bf16[1,1,128,3200]{2,3,1,0:T(8,128)(2,1)S(1)}, bf16[1,1,128,3200]{2,3,1,0:T(8,128)(2,1)S(1)}, u32[]{:S(2)}, u32[]{:S(2)}) collective-permute-start(bf16[1,1,128,3200]{2,3,1,0:T(8,128)(2,1)S(1)} %copy.15), channel_id=1, source_target_pairs={{0,4},{4,8},{8,12},{12,16},{16,20},{20,24},{24,28},{1,5},{5,9},{9,... | collective-permute-start | bytes 2457608 | tf_op jit(solution)/shard_map/ppermute | solution.py:16
  7.7 33.6 %collective-permute-done.1 = bf16[1,1,128,3200]{2,3,1,0:T(8,128)(2,1)S(1)} collective-permute-done((bf16[1,1,128,3200]{2,3,1,0:T(8,128)(2,1)S(1)}, bf16[1,1,128,3200]{2,3,1,0:T(8,128)(2,1)S(1)}, u32[]{:S(2)}, u32[]{:S(2)}) %collective-permute-start.1) | collective-permute-done | bytes 819232 | tf_op jit(solution)/shard_map/ppermute | solution.py:18
  41.3 0.9 copy-done.4
  42.2 1.7 pad_maximum_fusion
  43.9 1.9 %collective-permute-start.3 = (bf16[3,1,128,3200]{2,3,1,0:T(8,128)(2,1)}, bf16[3,1,128,3200]{2,3,1,0:T(8,128)(2,1)}, u32[]{:S(2)}, u32[]{:S(2)}) collective-permute-start(bf16[3,1,128,3200]{2,3,1,0:T(8,128)(2,1)} %pad_maximum_fusion), channel_id=1, source_target_pairs={{1,0},{2,1},{3,2},{5,4},{6,5},{7,6},{9,8},{10,9},{11,10},{13,12},{... | collective-permute-start | bytes 7372808 | tf_op jit(solution)/shard_map/ppermute | solution.py:18
  45.9 2.6 %copy.13 = bf16[1,8,1,128,1152]{3,4,2,0,1:T(8,128)(2,1)} copy(bf16[1,8,1,128,1152]{4,3,2,1,0:T(8,128)(2,1)S(1)} %copy-done.3) | data formatting | bytes 4718592 | tf_op args[0]
  48.4 5.5 %all-to-all-start = ((bf16[1,8,1,128,1152]{3,4,2,0,1:T(8,128)(2,1)}), bf16[1,8,1,128,1152]{3,4,2,0,1:T(8,128)(2,1)S(1)}, u32[]{:S(2)}, u32[]{:S(2)}) async-start(bf16[1,8,1,128,1152]{3,4,2,0,1:T(8,128)(2,1)} %copy.13), calls=%async_computation | async-start | bytes 4718592 | tf_op jit(solution)/shard_map/all_to_all | solution.py:37
  54.0 3.2 %collective-permute-start.2 = (bf16[3,1,128,3200]{2,3,1,0:T(8,128)(2,1)}, bf16[3,1,128,3200]{2,3,1,0:T(8,128)(2,1)}, u32[]{:S(2)}, u32[]{:S(2)}) collective-permute-start(bf16[3,1,128,3200]{2,3,1,0:T(8,128)(2,1)} %pad_maximum_fusion), channel_id=1, source_target_pairs={{0,1},{1,2},{2,3},{4,5},{5,6},{6,7},{8,9},{9,10},{10,11},{12,13},{... | collective-permute-start | bytes 7372808 | tf_op jit(solution)/shard_map/ppermute | solution.py:16
  57.3 1.0 slice.116
  58.3 1.7 slice.100
  60.0 13.6 %collective-permute-done.3 = bf16[3,1,128,3200]{2,3,1,0:T(8,128)(2,1)} collective-permute-done((bf16[3,1,128,3200]{2,3,1,0:T(8,128)(2,1)}, bf16[3,1,128,3200]{2,3,1,0:T(8,128)(2,1)}, u32[]{:S(2)}, u32[]{:S(2)}) %collective-permute-start.3) | collective-permute-done | bytes 2457632 | tf_op jit(solution)/shard_map/ppermute | solution.py:18
  73.6 1.8 fusion.27
  76.9 8.6 %collective-permute-done.2 = bf16[3,1,128,3200]{2,3,1,0:T(8,128)(2,1)} collective-permute-done((bf16[3,1,128,3200]{2,3,1,0:T(8,128)(2,1)}, bf16[3,1,128,3200]{2,3,1,0:T(8,128)(2,1)}, u32[]{:S(2)}, u32[]{:S(2)}) %collective-permute-start.2) | collective-permute-done | bytes 2457632 | tf_op jit(solution)/shard_map/ppermute | solution.py:16
  85.5 1.8 fusion.26
  89.5 17.2 %all-to-all-done = bf16[1,8,1,128,1152]{3,4,2,0,1:T(8,128)(2,1)S(1)} async-done(((bf16[1,8,1,128,1152]{3,4,2,0,1:T(8,128)(2,1)}), bf16[1,8,1,128,1152]{3,4,2,0,1:T(8,128)(2,1)S(1)}, u32[]{:S(2)}, u32[]{:S(2)}) %all-to-all-start) | async-done | bytes 2359328 | tf_op jit(solution)/shard_map/all_to_all | solution.py:37
  106.7 2.6 %copy.14 = bf16[1,8,1,128,1152]{4,3,1,2,0:T(8,128)(2,1)} copy(bf16[1,8,1,128,1152]{3,4,2,0,1:T(8,128)(2,1)S(1)} %all-to-all-done) | data formatting | bytes 4718592 | tf_op jit(solution)/shard_map/all_to_all | solution.py:37
  109.3 3.3 %bitcast_multiply_fusion = bf16[1024,1152]{1,0:T(8,128)(2,1)} fusion(bf16[1,8,1,128,1152]{4,3,1,2,0:T(8,128)(2,1)} %copy.14, bf16[1152]{0:T(1024)(128)(2,1)S(1)} %broadcast_bitcast_fusion), kind=kLoop, calls=%fused_computation.15 | loop fusion | flops 1179648 | bytes 4720896 | tf_op jit(solution)/shard_map/mul | solution.py:57
  112.6 2.2 %fusion.4 = bf16[8,1,1,128,1152]{3,4,0,2,1:T(8,128)(2,1)} fusion(bf16[1,8,1,128,1152]{3,4,2,0,1:T(8,128)(2,1)S(1)} %all-to-all-done, bf16[1152]{0:T(1024)(128)(2,1)S(1)} %broadcast_bitcast_fusion, bf16[1,1,128,128]{3,2,1,0:T(8,128)(2,1)S(1)} %copy-done), kind=kOutput, calls=%fused_computation.12 | convolution fusion | flops 304349184 | bytes 4753664 | tf_op jit(solution)/shard_map/ji,pabiw->pabjw/dot_general | solution.py:38
  114.8 4.3 %copy.19 = bf16[8,1,1,128,1152]{4,3,0,2,1:T(8,128)(2,1)} copy(bf16[8,1,1,128,1152]{3,4,0,2,1:T(8,128)(2,1)} %fusion.4) | data formatting | bytes 4718592 | tf_op jit(solution)/shard_map/mul | solution.py:58
  119.1 3.1 %copy.20 = bf16[1,8,128,1152]{3,1,2,0:T(8,128)(2,1)S(1)} copy(bf16[1,8,128,1152]{3,2,1,0:T(8,128)(2,1)} %bitcast.64) | data formatting | bytes 4718592
  123.3 0.8 fusion.14
  124.2 0.8 convolution_add_fusion.6
  125.2 0.8 convolution_add_fusion.5
  126.1 0.8 convolution_add_fusion.4
  126.9 0.8 convolution_add_fusion.3
  128.7 0.8 convolution_add_fusion.1
  129.5 2.2 %fusion.1 = bf16[1024,1152]{1,0:T(8,128)(2,1)} fusion(f32[1024,1152]{1,0:T(8,128)S(1)} %fusion.6, f32[1024,1152]{1,0:T(8,128)S(1)} %convolution_add_fusion.1, bf16[128,1152]{0,1:T(8,128)(2,1)S(1)} %bitcast.74, bf16[1024,1152]{1,0:T(8,128)(2,1)S(1)} %copy-done.2), kind=kOutput, calls=%fused_computation.8 | convolution fusion | flops 305528832 | bytes 12353536 | tf_op jit(solution)/shard_map/dot_general | solution.py:68
  131.7 4.1 %reshape.69 = bf16[8,147456]{1,0:T(8,128)(2,1)} reshape(bf16[1024,1152]{1,0:T(8,128)(2,1)} %fusion.1) | data formatting | bytes 4718592 | tf_op jit(solution)/shard_map/reshape | solution.py:69
  135.9 3.3 %fusion.28 = f32[8,8]{1,0:T(8,128)S(1)} fusion(bf16[8,147456]{1,0:T(8,128)(2,1)} %reshape.69, bf16[8,147456]{1,0:T(8,128)(2,1)S(1)} %bitcast.63), kind=kOutput, calls=%fused_computation.46 | convolution fusion | flops 18874368 | bytes 4718848 | tf_op jit(solution)/shard_map/dot_general | solution.py:71
  139.1 41.3 %psum.7 = f32[8,8]{1,0:T(8,128)S(1)} all-reduce(f32[8,8]{1,0:T(8,128)S(1)} %fusion.28), channel_id=1, replica_groups=mesh['row'=8,'col'=4] {'row','col'}, use_global_device_ids=true, to_apply=%region_0.1 | all-reduce | flops 64 | bytes 512 | tf_op jit(solution)/shard_map/psum | solution.py:75
  (38 shorter events, 6.9 us)
Async XLA Ops:
  0.0 112.6 %copy-start = (bf16[1,1,128,128]{3,2,1,0:T(8,128)(2,1)S(1)}, bf16[1,1,128,128]{3,2,1,0:T(8,128)(2,1)}, u32[]{:S(2)}) copy-start(bf16[1,1,128,128]{3,2,1,0:T(8,128)(2,1)} %param.7) | copy-start | bytes 98308
  1.7 44.1 %copy-start.3 = (bf16[1,8,1,128,1152]{4,3,2,1,0:T(8,128)(2,1)S(1)}, bf16[1,8,1,128,1152]{4,3,2,1,0:T(8,128)(2,1)}, u32[]{:S(2)}) copy-start(bf16[1,8,1,128,1152]{4,3,2,1,0:T(8,128)(2,1)} %param.4) | copy-start | bytes 7077892
  1.7 39.6 %collective-permute-start.1 = (bf16[1,1,128,3200]{2,3,1,0:T(8,128)(2,1)S(1)}, bf16[1,1,128,3200]{2,3,1,0:T(8,128)(2,1)S(1)}, u32[]{:S(2)}, u32[]{:S(2)}) collective-permute-start(bf16[1,1,128,3200]{2,3,1,0:T(8,128)(2,1)S(1)} %copy.15), channel_id=1, source_target_pairs={{4,0},{8,4},{12,8},{16,12},{20,16},{24,20},{28,24},{5,1},{9,5},{13... | collective-permute-start | bytes 2457608 | tf_op jit(solution)/shard_map/ppermute | solution.py:18
  5.2 36.1 %collective-permute-start = (bf16[1,1,128,3200]{2,3,1,0:T(8,128)(2,1)S(1)}, bf16[1,1,128,3200]{2,3,1,0:T(8,128)(2,1)S(1)}, u32[]{:S(2)}, u32[]{:S(2)}) collective-permute-start(bf16[1,1,128,3200]{2,3,1,0:T(8,128)(2,1)S(1)} %copy.15), channel_id=1, source_target_pairs={{0,4},{4,8},{8,12},{12,16},{16,20},{20,24},{24,28},{1,5},{5,9},{9,... | collective-permute-start | bytes 2457608 | tf_op jit(solution)/shard_map/ppermute | solution.py:16
  41.3 0.9 copy-start.4
  42.2 1.7 copy-start.5
  43.9 29.6 %collective-permute-start.3 = (bf16[3,1,128,3200]{2,3,1,0:T(8,128)(2,1)}, bf16[3,1,128,3200]{2,3,1,0:T(8,128)(2,1)}, u32[]{:S(2)}, u32[]{:S(2)}) collective-permute-start(bf16[3,1,128,3200]{2,3,1,0:T(8,128)(2,1)} %pad_maximum_fusion), channel_id=1, source_target_pairs={{1,0},{2,1},{3,2},{5,4},{6,5},{7,6},{9,8},{10,9},{11,10},{13,12},{... | collective-permute-start | bytes 7372808 | tf_op jit(solution)/shard_map/ppermute | solution.py:18
  48.4 8.8 %copy-start.12 = (s32[1,1,9]{2,1,0:T(1,128)S(1)}, s32[1,1,9]{2,1,0:T(1,128)}, u32[]{:S(2)}) copy-start(s32[1,1,9]{2,1,0:T(1,128)} %param.5) | copy-start | bytes 112
  48.4 58.3 %all-to-all-start = ((bf16[1,8,1,128,1152]{3,4,2,0,1:T(8,128)(2,1)}), bf16[1,8,1,128,1152]{3,4,2,0,1:T(8,128)(2,1)S(1)}, u32[]{:S(2)}, u32[]{:S(2)}) async-start(bf16[1,8,1,128,1152]{3,4,2,0,1:T(8,128)(2,1)} %copy.13), calls=%async_computation | async-start | bytes 4718592 | tf_op jit(solution)/shard_map/all_to_all | solution.py:37
  54.0 31.5 %collective-permute-start.2 = (bf16[3,1,128,3200]{2,3,1,0:T(8,128)(2,1)}, bf16[3,1,128,3200]{2,3,1,0:T(8,128)(2,1)}, u32[]{:S(2)}, u32[]{:S(2)}) collective-permute-start(bf16[3,1,128,3200]{2,3,1,0:T(8,128)(2,1)} %pad_maximum_fusion), channel_id=1, source_target_pairs={{0,1},{1,2},{2,3},{4,5},{5,6},{6,7},{8,9},{9,10},{10,11},{12,13},{... | collective-permute-start | bytes 7372808 | tf_op jit(solution)/shard_map/ppermute | solution.py:16
  119.1 3.1 %copy-start.2 = (bf16[1024,1152]{1,0:T(8,128)(2,1)S(1)}, bf16[1024,1152]{1,0:T(8,128)(2,1)}, u32[]{:S(2)}) copy-start(bf16[1024,1152]{1,0:T(8,128)(2,1)} %bitcast_multiply_fusion) | copy-start | bytes 7077892
  119.1 3.1 %copy-start.9 = (bf16[128,3,3,128]{0,3,2,1:T(8,128)(2,1)S(1)}, bf16[128,3,3,128]{0,3,2,1:T(8,128)(2,1)}, u32[]{:S(2)}) copy-start(bf16[128,3,3,128]{0,3,2,1:T(8,128)(2,1)} %slice.119) | copy-start | bytes 884740
  122.3 1.0 copy-start.6
  123.3 1.0 copy-start.11
  124.2 1.0 copy-start.8
  125.2 1.0 copy-start.10
  127.7 1.0 copy-start.7
  131.7 49.4 %copy-start.1 = (bf16[1,1,128,128]{3,2,1,0:T(8,128)(2,1)S(1)}, bf16[1,1,128,128]{3,2,1,0:T(8,128)(2,1)}, u32[]{:S(2)}) copy-start(bf16[1,1,128,128]{3,2,1,0:T(8,128)(2,1)} %param.7) | copy-start | bytes 98308
where the time goes:
time: 182 us; the launch traced here: 181 us
  waiting for transfers between devices  72.9 us (40%)
  blocking collectives  41.3 us (23%)
  local copies, waits for them, and re-layouts  30.4 us (17%)
  starting transfers between devices  16.6 us (9%)
  matrix products  14 us (8%)
  other arithmetic  5.65 us (3%)
    ppermute x2, waiting for transfers between devices, extended(): lax.ppermute(head, axis, [((i + 1) % count, i) for i in range(ends)])  47.1 us
    psum x1, blocking collectives, per_device(): response = lax.psum(partial_value, ('row', 'col'))  41.3 us
    all_to_all x1, waiting for transfers between devices, per_device(): lax.all_to_all(tensor_ri, 'row', split_axis=1, concat_axis=0, tiled=True)  17.2 us
    unnamed x29, local copies, waits for them, and re-layouts  9.19 us
    ppermute x2, waiting for transfers between devices, extended(): lax.ppermute(tail, axis, [(i, (i + 1) % count) for i in range(ends)])  8.6 us
    dot_general x9, matrix products, per_device(): jnp.dot(tile, windows[source], preferred_element_type=jnp.float32)  8.5 us
    slice x9, local copies, waits for them, and re-layouts, window_of(): picked = grid_band[:, 2 - src_row:5 - src_row, 2 - src_col:5 - src_col, :]  6.45 us
    ppermute x2, starting transfers between devices, extended(): lax.ppermute(tail, axis, [(i, (i + 1) % count) for i in range(ends)])  5.74 us
  transfers between devices with their start and end apart: 5, of which 4 were waited for; matrix products, arithmetic and copies ran while one was open for 7% of the time, Pallas kernels for 0%

commit v1 on v0

--- a/solution.py
+++ b/solution.py
@@ -72,7 +72,7 @@
         half_done, occ_flat, (((1,), (1,)), ((), ())), preferred_element_type=jnp.float32
     )
     total_basis = block_width * row_count * col_count
-    response = lax.psum(partial_value, ("row", "col"))
+    response = lax.psum(lax.psum(partial_value, "col"), "row")
     return response * (1.0 / math.sqrt(total_basis * 9 * block_width))
 
 

time: 182 us -> 170 us (0.934)
  the two profiles are of different devices: /device:TPU:10 before, /device:TPU:0 now
where the time goes in v1:
time: 170 us; the launch traced here: 169 us
  waiting for transfers between devices  75 us (44%)
  local copies, waits for them, and re-layouts  29.4 us (17%)
  blocking collectives  26.9 us (16%)
  starting transfers between devices  18.4 us (11%)
  matrix products  14 us (8%)
  other arithmetic  5.65 us (3%)
    all_to_all x1, waiting for transfers between devices, per_device(): lax.all_to_all(tensor_ri, 'row', split_axis=1, concat_axis=0, tiled=True)  41.1 us
    psum x2, blocking collectives, per_device(): response = lax.psum(lax.psum(partial_value, 'col'), 'row')  26.9 us
    ppermute x2, waiting for transfers between devices, extended(): lax.ppermute(tail, axis, [(i, (i + 1) % count) for i in range(ends)])  17.7 us
    ppermute x2, waiting for transfers between devices, extended(): lax.ppermute(head, axis, [((i + 1) % count, i) for i in range(ends)])  16.3 us
    ppermute x2, starting transfers between devices, extended(): lax.ppermute(tail, axis, [(i, (i + 1) % count) for i in range(ends)])  9.76 us
    dot_general x9, matrix products, per_device(): jnp.dot(tile, windows[source], preferred_element_type=jnp.float32)  8.48 us
    unnamed x29, local copies, waits for them, and re-layouts  8.25 us
    slice x9, local copies, waits for them, and re-layouts, window_of(): picked = grid_band[:, 2 - src_row:5 - src_row, 2 - src_col:5 - src_col, :]  6.39 us
  transfers between devices with their start and end apart: 5, of which 3 were waited for; matrix products, arithmetic and copies ran while one was open for 7% of the time, Pallas kernels for 0%

profile of v1, /device:TPU:0, one launch (start us, length us, event | category | flops | bytes accessed | tf_op | source)
XLA Modules:
  0.0 169.5 jit_solution(1971614817432485545)
XLA Ops:
  0.0 1.7 %copy.15 = bf16[1,1,128,3200]{2,3,1,0:T(8,128)(2,1)S(1)} copy(bf16[1,1,128,3200]{3,2,1,0:T(8,128)(2,1)} %param.6) | data formatting | bytes 1638400 | tf_op args[2]
  1.7 1.4 collective-permute-start.1
  3.2 5.6 %collective-permute-start = (bf16[1,1,128,3200]{2,3,1,0:T(8,128)(2,1)S(1)}, bf16[1,1,128,3200]{2,3,1,0:T(8,128)(2,1)S(1)}, u32[]{:S(2)}, u32[]{:S(2)}) collective-permute-start(bf16[1,1,128,3200]{2,3,1,0:T(8,128)(2,1)S(1)} %copy.15), channel_id=1, source_target_pairs={{0,4},{4,8},{8,12},{12,16},{16,20},{20,24},{24,28},{1,5},{5,9},{9,... | collective-permute-start | bytes 2457608 | tf_op jit(solution)/shard_map/ppermute | solution.py:16
  8.7 16.3 %collective-permute-done.1 = bf16[1,1,128,3200]{2,3,1,0:T(8,128)(2,1)S(1)} collective-permute-done((bf16[1,1,128,3200]{2,3,1,0:T(8,128)(2,1)S(1)}, bf16[1,1,128,3200]{2,3,1,0:T(8,128)(2,1)S(1)}, u32[]{:S(2)}, u32[]{:S(2)}) %collective-permute-start.1) | collective-permute-done | bytes 819232 | tf_op jit(solution)/shard_map/ppermute | solution.py:18
  25.0 17.7 %collective-permute-done = bf16[1,1,128,3200]{2,3,1,0:T(8,128)(2,1)S(1)} collective-permute-done((bf16[1,1,128,3200]{2,3,1,0:T(8,128)(2,1)S(1)}, bf16[1,1,128,3200]{2,3,1,0:T(8,128)(2,1)S(1)}, u32[]{:S(2)}, u32[]{:S(2)}) %collective-permute-start) | collective-permute-done | bytes 819232 | tf_op jit(solution)/shard_map/ppermute | solution.py:16
  42.7 1.7 %pad_maximum_fusion = bf16[3,1,128,3200]{2,3,1,0:T(8,128)(2,1)} fusion(bf16[1,1,128,3200]{2,3,1,0:T(8,128)(2,1)S(1)} %collective-permute-done.1, bf16[1,1,128,3200]{2,3,1,0:T(8,128)(2,1)S(1)} %copy.15, bf16[1,1,128,3200]{2,3,1,0:T(8,128)(2,1)S(1)} %collective-permute-done), kind=kLoop, calls=%fused_computation.13 | loop fusion | flops 2457600 | bytes 4915200 | tf_op jit(solution)/shard_map/concatenate | solution.py:14
  44.4 1.3 collective-permute-start.3
  45.7 2.5 %copy.13 = bf16[1,8,1,128,1152]{3,4,2,0,1:T(8,128)(2,1)} copy(bf16[1,8,1,128,1152]{4,3,2,1,0:T(8,128)(2,1)S(1)} %copy-done.3) | data formatting | bytes 4718592 | tf_op args[0]
  48.2 6.0 %all-to-all-start = ((bf16[1,8,1,128,1152]{3,4,2,0,1:T(8,128)(2,1)}), bf16[1,8,1,128,1152]{3,4,2,0,1:T(8,128)(2,1)S(1)}, u32[]{:S(2)}, u32[]{:S(2)}) async-start(bf16[1,8,1,128,1152]{3,4,2,0,1:T(8,128)(2,1)} %copy.13), calls=%async_computation | async-start | bytes 4718592 | tf_op jit(solution)/shard_map/all_to_all | solution.py:37
  54.2 4.2 %collective-permute-start.2 = (bf16[3,1,128,3200]{2,3,1,0:T(8,128)(2,1)}, bf16[3,1,128,3200]{2,3,1,0:T(8,128)(2,1)}, u32[]{:S(2)}, u32[]{:S(2)}) collective-permute-start(bf16[3,1,128,3200]{2,3,1,0:T(8,128)(2,1)} %pad_maximum_fusion), channel_id=1, source_target_pairs={{0,1},{1,2},{2,3},{4,5},{5,6},{6,7},{8,9},{9,10},{10,11},{12,13},{... | collective-permute-start | bytes 7372808 | tf_op jit(solution)/shard_map/ppermute | solution.py:16
  58.5 1.0 slice.116
  59.5 1.7 %slice.100 = bf16[128,3,3,128]{0,3,2,1:T(8,128)(2,1)} slice(bf16[128,5,5,128]{0,3,2,1:T(8,128)(2,1)} %bitcast.67), slice={[0:128], [2:5], [1:4], [0:128]} | slice | bytes 589824 | tf_op jit(solution)/shard_map/slice | solution.py:27
  61.2 1.8 %fusion.27 = (bf16[1,1,128,3200]{2,3,1,0:T(8,128)(2,1)S(1)}, bf16[1,1,128,3200]{2,3,1,0:T(8,128)(2,1)S(1)}, bf16[1,1,128,3200]{2,3,1,0:T(8,128)(2,1)S(1)}) fusion(bf16[3,1,128,3200]{2,3,1,0:T(8,128)(2,1)} %collective-permute-done.3), kind=kLoop, calls=%fused_computation.45 | loop fusion | bytes 4915200 | tf_op jit(solution)/shard_map/slice | solution.py:63
  64.5 1.8 %fusion.26 = (bf16[1,1,128,3200]{2,3,1,0:T(8,128)(2,1)S(1)}, bf16[1,1,128,3200]{2,3,1,0:T(8,128)(2,1)S(1)}, bf16[1,1,128,3200]{2,3,1,0:T(8,128)(2,1)S(1)}) fusion(bf16[3,1,128,3200]{2,3,1,0:T(8,128)(2,1)} %collective-permute-done.2), kind=kLoop, calls=%fused_computation.44 | loop fusion | bytes 4915200 | tf_op jit(solution)/shard_map/slice | solution.py:63
  68.5 41.1 %all-to-all-done = bf16[1,8,1,128,1152]{3,4,2,0,1:T(8,128)(2,1)S(1)} async-done(((bf16[1,8,1,128,1152]{3,4,2,0,1:T(8,128)(2,1)}), bf16[1,8,1,128,1152]{3,4,2,0,1:T(8,128)(2,1)S(1)}, u32[]{:S(2)}, u32[]{:S(2)}) %all-to-all-start) | async-done | bytes 2359328 | tf_op jit(solution)/shard_map/all_to_all | solution.py:37
  109.6 2.5 %copy.14 = bf16[1,8,1,128,1152]{4,3,1,2,0:T(8,128)(2,1)} copy(bf16[1,8,1,128,1152]{3,4,2,0,1:T(8,128)(2,1)S(1)} %all-to-all-done) | data formatting | bytes 4718592 | tf_op jit(solution)/shard_map/all_to_all | solution.py:37
  112.1 3.3 %bitcast_multiply_fusion = bf16[1024,1152]{1,0:T(8,128)(2,1)} fusion(bf16[1,8,1,128,1152]{4,3,1,2,0:T(8,128)(2,1)} %copy.14, bf16[1152]{0:T(1024)(128)(2,1)S(1)} %broadcast_bitcast_fusion), kind=kLoop, calls=%fused_computation.15 | loop fusion | flops 1179648 | bytes 4720896 | tf_op jit(solution)/shard_map/mul | solution.py:57
  115.4 2.2 %fusion.4 = bf16[8,1,1,128,1152]{3,4,0,2,1:T(8,128)(2,1)} fusion(bf16[1,8,1,128,1152]{3,4,2,0,1:T(8,128)(2,1)S(1)} %all-to-all-done, bf16[1152]{0:T(1024)(128)(2,1)S(1)} %broadcast_bitcast_fusion, bf16[1,1,128,128]{3,2,1,0:T(8,128)(2,1)S(1)} %copy-done), kind=kOutput, calls=%fused_computation.12 | convolution fusion | flops 304349184 | bytes 4753664 | tf_op jit(solution)/shard_map/ji,pabiw->pabjw/dot_general | solution.py:38
  117.7 4.3 %copy.19 = bf16[8,1,1,128,1152]{4,3,0,2,1:T(8,128)(2,1)} copy(bf16[8,1,1,128,1152]{3,4,0,2,1:T(8,128)(2,1)} %fusion.4) | data formatting | bytes 4718592 | tf_op jit(solution)/shard_map/mul | solution.py:58
  122.0 3.1 %copy.20 = bf16[1,8,128,1152]{3,1,2,0:T(8,128)(2,1)S(1)} copy(bf16[1,8,128,1152]{3,2,1,0:T(8,128)(2,1)} %bitcast.64) | data formatting | bytes 4718592
  125.2 0.8 fusion.6
  127.1 0.8 convolution_add_fusion.6
  128.0 0.8 convolution_add_fusion.5
  129.0 0.8 convolution_add_fusion.4
  129.8 0.8 convolution_add_fusion.3
  130.6 0.8 convolution_add_fusion.2
  131.6 0.8 convolution_add_fusion.1
  132.4 2.2 %fusion.1 = bf16[1024,1152]{1,0:T(8,128)(2,1)} fusion(f32[1024,1152]{1,0:T(8,128)S(1)} %fusion.6, f32[1024,1152]{1,0:T(8,128)S(1)} %convolution_add_fusion.1, bf16[128,1152]{0,1:T(8,128)(2,1)S(1)} %bitcast.74, bf16[1024,1152]{1,0:T(8,128)(2,1)S(1)} %copy-done.2), kind=kOutput, calls=%fused_computation.8 | convolution fusion | flops 305528832 | bytes 12353536 | tf_op jit(solution)/shard_map/dot_general | solution.py:68
  134.6 4.2 %reshape.69 = bf16[8,147456]{1,0:T(8,128)(2,1)} reshape(bf16[1024,1152]{1,0:T(8,128)(2,1)} %fusion.1) | data formatting | bytes 4718592 | tf_op jit(solution)/shard_map/reshape | solution.py:69
  138.7 3.3 %fusion.28 = f32[8,8]{1,0:T(8,128)S(1)} fusion(bf16[8,147456]{1,0:T(8,128)(2,1)} %reshape.69, bf16[8,147456]{1,0:T(8,128)(2,1)S(1)} %bitcast.63), kind=kOutput, calls=%fused_computation.46 | convolution fusion | flops 18874368 | bytes 4718848 | tf_op jit(solution)/shard_map/dot_general | solution.py:71
  142.0 7.6 %psum.14 = f32[8,8]{1,0:T(8,128)S(1)} all-reduce(f32[8,8]{1,0:T(8,128)S(1)} %fusion.28), channel_id=1, replica_groups=mesh['row'=8,'col'=4] {'col'}, use_global_device_ids=true, to_apply=%region_0.1 | all-reduce | flops 64 | bytes 512 | tf_op jit(solution)/shard_map/psum | solution.py:75
  149.6 19.3 %psum.15 = f32[8,8]{1,0:T(8,128)S(1)} all-reduce(f32[8,8]{1,0:T(8,128)S(1)} %psum.14), channel_id=1, replica_groups=mesh['row'=8,'col'=4] {'row'}, use_global_device_ids=true, to_apply=%region_1.2 | all-reduce | flops 64 | bytes 512 | tf_op jit(solution)/shard_map/psum | solution.py:75
  (39 shorter events, 6.1 us)
Async XLA Ops:
  0.0 115.4 %copy-start = (bf16[1,1,128,128]{3,2,1,0:T(8,128)(2,1)S(1)}, bf16[1,1,128,128]{3,2,1,0:T(8,128)(2,1)}, u32[]{:S(2)}) copy-start(bf16[1,1,128,128]{3,2,1,0:T(8,128)(2,1)} %param.7) | copy-start | bytes 98308
  1.7 44.0 %copy-start.3 = (bf16[1,8,1,128,1152]{4,3,2,1,0:T(8,128)(2,1)S(1)}, bf16[1,8,1,128,1152]{4,3,2,1,0:T(8,128)(2,1)}, u32[]{:S(2)}) copy-start(bf16[1,8,1,128,1152]{4,3,2,1,0:T(8,128)(2,1)} %param.4) | copy-start | bytes 7077892
  1.7 23.2 %collective-permute-start.1 = (bf16[1,1,128,3200]{2,3,1,0:T(8,128)(2,1)S(1)}, bf16[1,1,128,3200]{2,3,1,0:T(8,128)(2,1)S(1)}, u32[]{:S(2)}, u32[]{:S(2)}) collective-permute-start(bf16[1,1,128,3200]{2,3,1,0:T(8,128)(2,1)S(1)} %copy.15), channel_id=1, source_target_pairs={{4,0},{8,4},{12,8},{16,12},{20,16},{24,20},{28,24},{5,1},{9,5},{13... | collective-permute-start | bytes 2457608 | tf_op jit(solution)/shard_map/ppermute | solution.py:18
  3.2 39.5 %collective-permute-start = (bf16[1,1,128,3200]{2,3,1,0:T(8,128)(2,1)S(1)}, bf16[1,1,128,3200]{2,3,1,0:T(8,128)(2,1)S(1)}, u32[]{:S(2)}, u32[]{:S(2)}) collective-permute-start(bf16[1,1,128,3200]{2,3,1,0:T(8,128)(2,1)S(1)} %copy.15), channel_id=1, source_target_pairs={{0,4},{4,8},{8,12},{12,16},{16,20},{20,24},{24,28},{1,5},{5,9},{9,... | collective-permute-start | bytes 2457608 | tf_op jit(solution)/shard_map/ppermute | solution.py:16
  25.0 17.7 %copy-start.4 = (bf16[1,1,128,3200]{2,3,1,0:T(8,128)(2,1)}, bf16[1,1,128,3200]{2,3,1,0:T(8,128)(2,1)S(1)}, u32[]{:S(2)}) copy-start(bf16[1,1,128,3200]{2,3,1,0:T(8,128)(2,1)S(1)} %collective-permute-done.1) | copy-start | bytes 2457604
  42.7 1.7 %copy-start.5 = (bf16[1,1,128,3200]{2,3,1,0:T(8,128)(2,1)}, bf16[1,1,128,3200]{2,3,1,0:T(8,128)(2,1)S(1)}, u32[]{:S(2)}) copy-start(bf16[1,1,128,3200]{2,3,1,0:T(8,128)(2,1)S(1)} %collective-permute-done) | copy-start | bytes 2457604
  44.4 16.8 %collective-permute-start.3 = (bf16[3,1,128,3200]{2,3,1,0:T(8,128)(2,1)}, bf16[3,1,128,3200]{2,3,1,0:T(8,128)(2,1)}, u32[]{:S(2)}, u32[]{:S(2)}) collective-permute-start(bf16[3,1,128,3200]{2,3,1,0:T(8,128)(2,1)} %pad_maximum_fusion), channel_id=1, source_target_pairs={{1,0},{2,1},{3,2},{5,4},{6,5},{7,6},{9,8},{10,9},{11,10},{13,12},{... | collective-permute-start | bytes 7372808 | tf_op jit(solution)/shard_map/ppermute | solution.py:18
  48.2 10.2 %copy-start.12 = (s32[1,1,9]{2,1,0:T(1,128)S(1)}, s32[1,1,9]{2,1,0:T(1,128)}, u32[]{:S(2)}) copy-start(s32[1,1,9]{2,1,0:T(1,128)} %param.5) | copy-start | bytes 112
  48.2 61.4 %all-to-all-start = ((bf16[1,8,1,128,1152]{3,4,2,0,1:T(8,128)(2,1)}), bf16[1,8,1,128,1152]{3,4,2,0,1:T(8,128)(2,1)S(1)}, u32[]{:S(2)}, u32[]{:S(2)}) async-start(bf16[1,8,1,128,1152]{3,4,2,0,1:T(8,128)(2,1)} %copy.13), calls=%async_computation | async-start | bytes 4718592 | tf_op jit(solution)/shard_map/all_to_all | solution.py:37
  54.2 10.3 %collective-permute-start.2 = (bf16[3,1,128,3200]{2,3,1,0:T(8,128)(2,1)}, bf16[3,1,128,3200]{2,3,1,0:T(8,128)(2,1)}, u32[]{:S(2)}, u32[]{:S(2)}) collective-permute-start(bf16[3,1,128,3200]{2,3,1,0:T(8,128)(2,1)} %pad_maximum_fusion), channel_id=1, source_target_pairs={{0,1},{1,2},{2,3},{4,5},{5,6},{6,7},{8,9},{9,10},{10,11},{12,13},{... | collective-permute-start | bytes 7372808 | tf_op jit(solution)/shard_map/ppermute | solution.py:16
  122.0 3.1 %copy-start.2 = (bf16[1024,1152]{1,0:T(8,128)(2,1)S(1)}, bf16[1024,1152]{1,0:T(8,128)(2,1)}, u32[]{:S(2)}) copy-start(bf16[1024,1152]{1,0:T(8,128)(2,1)} %bitcast_multiply_fusion) | copy-start | bytes 7077892
  122.0 3.1 %copy-start.9 = (bf16[128,3,3,128]{0,3,2,1:T(8,128)(2,1)S(1)}, bf16[128,3,3,128]{0,3,2,1:T(8,128)(2,1)}, u32[]{:S(2)}) copy-start(bf16[128,3,3,128]{0,3,2,1:T(8,128)(2,1)} %slice.119) | copy-start | bytes 884740
  125.2 1.0 copy-start.6
  126.1 1.0 copy-start.11
  127.1 1.0 copy-start.8
  128.0 1.0 copy-start.10
  130.6 1.0 copy-start.7
  134.6 34.9 %copy-start.1 = (bf16[1,1,128,128]{3,2,1,0:T(8,128)(2,1)S(1)}, bf16[1,1,128,128]{3,2,1,0:T(8,128)(2,1)}, u32[]{:S(2)}) copy-start(bf16[1,1,128,128]{3,2,1,0:T(8,128)(2,1)} %param.7) | copy-start | bytes 98308
